TPU v7x, 512 devices: a whole 4x4x16 slice. The times are simulated.
512 devices in a mesh: rows: 32 (over y, z_lo, core), cols: 16 (over x, z_hi).
Axes of the slice: x: 4, y: 4, z: 16 (z_hi: 4, z_lo: 4; z = z_hi * 4 + z_lo), core: 2. Of those that a mesh axis runs over, the one named last changes fastest.
Arguments:
- points: float32 [16384, 256], P('rows'), may hold values from -4 to 4, as said below
- centers: float32 [16384, 256], P('cols'), may hold values from -4 to 4, as said below
- inv_factor: float32 [16384, 16384], P('cols', 'rows'), may hold values from -2 to 2, as said below
- solution: float32 [16384, 128], P('rows'), may hold values from -6 to 6
- residual: float32 [16384, 128], P('rows'), may hold values from -40 to 40
- direction: float32 [16384, 128], P('rows'), may hold values from -40 to 40
Outputs:
- new_solution: float32 [16384, 128], P('rows')
- new_residual: float32 [16384, 128], P('rows')
- new_direction: float32 [16384, 128], P('rows')
Inputs may be any that keep to these rules, and one draw needn't show every extreme that they name: `points`: each point's coordinates have a fixed spread that differs from coordinate to coordinate. `centers`: drawn by the same law as points. `inv_factor`: upper triangular with a positive diagonal.
All inputs are finite; a program needn't handle non-finite values.
Results may differ from a plain program's by a relative error of at most 0.00027.
Values sent between devices are 32-bit elements; how exact they have to be, the bound alone decides.
A program may use at most 64 MiB of HBM per device.

v0:
```python
import jax
import jax.numpy as jnp
from jax import lax
from jax.sharding import PartitionSpec as P

ridge_weight = 0.02


def padded_to(lines, devices):
    spare = -lines.shape[0] % devices
    if not spare:
        return lines
    return jnp.concatenate([lines, jnp.zeros((spare, *lines.shape[1:]), lines.dtype)])


def joined_along(parts, dim):
    lengths = list(parts.shape[1:])
    lengths[dim] *= parts.shape[0]
    return jnp.moveaxis(parts, 0, dim).reshape(lengths)


def from_everyone(value, axis):
    devices = lax.axis_size(axis)
    return lax.all_to_all(
        jnp.broadcast_to(value[None], (devices, *value.shape)), axis, 0, 0, tiled=True
    )


def gather_directly(value, axis, dim):
    return joined_along(from_everyone(value, axis), dim)


def in_blocks(value, dim, devices):
    lengths = value.shape
    parts = value.reshape(*lengths[:dim], devices, lengths[dim] // devices, *lengths[dim + 1 :])
    return jnp.moveaxis(parts, dim, 0)


def summed_on_arrival(value, axis, dim):
    parts = in_blocks(value, dim, lax.axis_size(axis))
    arrived = lax.all_to_all(parts, axis, split_axis=0, concat_axis=0, tiled=True)
    return arrived.sum(axis=0)


def sum_by_parts(value, axes):
    padded = padded_to(value, lax.axis_size(axes))
    whole = gather_directly(summed_on_arrival(padded, axes, 0), axes, 0)
    return lax.slice_in_dim(whole, 0, len(value)).reshape(value.shape)


def packed_total(arrays, axis):
    ends = [0]
    for a in arrays:
        ends.append(ends[-1] + a.size)
    subtotal = sum_by_parts(jnp.concatenate([a.ravel() for a in arrays]), axis)
    return tuple((subtotal[b:e].reshape(a.shape) for a, b, e in zip(arrays, ends, ends[1:])))


def sum_by_parts_2(value, axes):
    lines = value.reshape(-1, value.shape[-1])
    padded = padded_to(lines, lax.axis_size(axes))
    whole = gather_directly(summed_on_arrival(padded, axes, 0), axes, 0)
    return lax.slice_in_dim(whole, 0, len(lines)).reshape(value.shape)


def of_everyone(value, axis):
    return from_everyone(value, axis).sum(axis=0)


def body(points, centers, inv_factor, solution, residual, direction):
    highest = lax.Precision.HIGHEST
    mapped_part = jnp.dot(
        inv_factor, direction, precision=highest, preferred_element_type=jnp.float32
    )
    norm_part = jnp.sum(residual * residual, axis=0)
    square_part = jnp.sum(direction * direction, axis=0)
    mapped, norm_now, dir_norm = packed_total((mapped_part, norm_part, square_part), "rows")
    point_sq = jnp.sum(points * points, axis=1)
    center_sq = jnp.sum(centers * centers, axis=1)
    inner_products = lax.dot_general(
        points,
        centers,
        (((1,), (1,)), ((), ())),
        precision=highest,
        preferred_element_type=jnp.float32,
    )
    kernel = jnp.exp(-0.5 * (point_sq[:, None] + center_sq[None, :] - 2.0 * inner_products))
    predicted_part = jnp.dot(kernel, mapped, precision=highest, preferred_element_type=jnp.float32)
    predicted = sum_by_parts_2(predicted_part, "cols")
    back_part = lax.dot_general(
        kernel,
        predicted,
        (((0,), (0,)), ((), ())),
        precision=highest,
        preferred_element_type=jnp.float32,
    )
    pred_norm = jnp.sum(predicted * predicted, axis=0)
    back, pred_total = packed_total((back_part, pred_norm), "rows")
    image_part = lax.dot_general(
        inv_factor,
        back,
        (((0,), (0,)), ((), ())),
        precision=highest,
        preferred_element_type=jnp.float32,
    )
    image = sum_by_parts_2(image_part, "cols") + ridge_weight * direction
    curvature = pred_total + ridge_weight * dir_norm
    step_size = norm_now / curvature
    new_solution = solution + step_size[None, :] * direction
    new_residual = residual - step_size[None, :] * image
    norm_next = of_everyone(jnp.sum(new_residual * new_residual, axis=0), "rows")
    new_direction = new_residual + (norm_next / norm_now)[None, :] * direction
    return (new_solution, new_residual, new_direction)


def solution(mesh):
    return jax.shard_map(
        body,
        mesh=mesh,
        in_specs=(
            P("rows", None),
            P("cols", None),
            P("cols", "rows"),
            P("rows", None),
            P("rows", None),
            P("rows", None),
        ),
        out_specs=(P("rows", None), P("rows", None), P("rows", None)),
        check_vma=False,
    )
```

profile of v0, /device:TPU:1, one launch (start us, length us, event | category | flops | bytes accessed | tf_op | source)
XLA Modules:
  0.0 257.6 jit_solution(6483939283104088810)
XLA Ops:
  0.6 1.3 multiply_reduce_fusion.4
  2.4 2.7 %convolution_bitcast_fusion.1 = f32[131072]{0:T(1024)S(1)} fusion(f32[1024,512]{1,0:T(8,128)S(1)} %copy-done, f32[512,128]{1,0:T(8,128)} %param.11), kind=kOutput, calls=%fused_computation.1 | convolution fusion | flops 805306368 | bytes 2883584 | tf_op jit(solution)/shard_map/dot_general | solution.py:72
  5.2 1.5 all_to_all.36
  6.7 28.4 %all_to_all.56 = f32[32,1,4104]{2,1,0:T(1,128)} all-to-all(f32[32,1,4104]{2,1,0:T(1,128)} %all_to_all.36), channel_id=1, replica_groups=mesh['rows'=32,'cols'=16] {'rows'}, dimensions={0} | all-to-all | bytes 1050624 | tf_op jit(solution)/shard_map/all_to_all | solution.py:41
  35.1 1.4 reduce_sum.101
  36.5 1.1 broadcast_in_dim.10
  37.6 4.4 %all-to-all-start.1 = ((f32[32,1,4104]{2,1,0:T(1,128)}), f32[32,1,4104]{2,1,0:T(1,128)}, u32[]{:S(2)}, u32[]{:S(2)}) async-start(f32[32,1,4104]{2,1,0:T(1,128)} %broadcast_in_dim.10), calls=%async_computation.1 | async-start | bytes 1081344 | tf_op jit(solution)/shard_map/all_to_all | solution.py:24
  42.0 1.2 multiply_reduce_fusion.1
  43.4 4.6 %multiply_exponential_fusion = f32[512,1024]{1,0:T(8,128)} fusion(f32[512,256]{1,0:T(8,128)} %param.6, f32[1024,256]{1,0:T(8,128)S(1)} %copy-done.1, f32[1024]{0:T(1024)S(1)} %multiply_reduce_fusion, f32[512]{0:T(512)S(1)} %multiply_reduce_fusion.1), kind=kOutput, calls=%fused_computation.2 | convolution fusion | flops 1612709888 | bytes 3676160 | tf_op jit(solution)/shard_map/dot_general | solution.py:80
  48.0 11.1 %all-to-all-done.1 = f32[32,1,4104]{2,1,0:T(1,128)} async-done(((f32[32,1,4104]{2,1,0:T(1,128)}), f32[32,1,4104]{2,1,0:T(1,128)}, u32[]{:S(2)}, u32[]{:S(2)}) %all-to-all-start.1) | async-done | bytes 525344 | tf_op jit(solution)/shard_map/all_to_all | solution.py:24
  59.2 2.3 reduce.4
  61.7 3.4 %fusion.1 = f32[16,32,128]{2,1,0:T(8,128)S(1)} fusion(f32[16,32,1024]{2,1,0:T(8,128)} %bitcast.28, f32[1026,128]{1,0:T(8,128)S(1)} %slice.22), kind=kOutput, calls=%fused_computation.9 | convolution fusion | flops 805306368 | bytes 2883584 | tf_op jit(solution)/shard_map/dot_general | solution.py:88
  65.1 33.7 %all_to_all.57 = f32[16,32,128]{2,1,0:T(8,128)S(1)} all-to-all(f32[16,32,128]{2,1,0:T(8,128)S(1)} %fusion.1), channel_id=1, replica_groups=mesh['rows'=32,'cols'=16] {'cols'}, dimensions={0} | all-to-all | bytes 524288 | tf_op jit(solution)/shard_map/all_to_all | solution.py:41
  98.9 21.5 %all_to_all.58 = f32[16,32,128]{2,1,0:T(8,128)S(1)} all-to-all(f32[16,32,128]{2,1,0:T(8,128)S(1)} %broadcast_in_dim.11), channel_id=1, replica_groups=mesh['rows'=32,'cols'=16] {'cols'}, dimensions={0} | all-to-all | bytes 524288 | tf_op jit(solution)/shard_map/all_to_all | solution.py:24
  120.3 5.0 %convolution_bitcast_fusion = f32[131072]{0:T(1024)S(1)} fusion(f32[512,1024]{1,0:T(8,128)} %multiply_exponential_fusion, f32[512,128]{1,0:T(8,128)S(1)} %bitcast.29), kind=kOutput, calls=%fused_computation | convolution fusion | flops 805306368 | bytes 2883584 | tf_op jit(solution)/shard_map/dot_general | solution.py:90
  125.4 0.8 pad_maximum_fusion.1
  126.3 1.8 all_to_all.41
  128.1 28.8 %all_to_all.59 = f32[32,1,4100]{2,1,0:T(1,128)} all-to-all(f32[32,1,4100]{2,1,0:T(1,128)S(1)} %all_to_all.41), channel_id=1, replica_groups=mesh['rows'=32,'cols'=16] {'rows'}, dimensions={0} | all-to-all | bytes 1049600 | tf_op jit(solution)/shard_map/all_to_all | solution.py:41
  156.9 1.4 reduce_sum.106
  158.5 20.7 %all_to_all.60 = f32[32,1,4100]{2,1,0:T(1,128)} all-to-all(f32[32,1,4100]{2,1,0:T(1,128)S(1)} %broadcast_in_dim.12), channel_id=1, replica_groups=mesh['rows'=32,'cols'=16] {'rows'}, dimensions={0} | all-to-all | bytes 1049600 | tf_op jit(solution)/shard_map/all_to_all | solution.py:24
  179.3 2.3 reduce.6
  181.6 1.0 slice.26
  182.6 3.1 %convolution_bitcast_fusion.2 = f32[512,128]{0,1:T(8,128)} fusion(f32[1024,512]{1,0:T(8,128)S(1)} %copy-done, f32[1025,128]{1,0:T(8,128)} %slice.26), kind=kOutput, calls=%fused_computation.3 | convolution fusion | flops 805306368 | bytes 2883584 | tf_op jit(solution)/shard_map/dot_general | solution.py:99
  185.8 1.8 copy.14
  187.6 24.1 %all_to_all.61 = f32[16,32,128]{2,1,0:T(8,128)} all-to-all(f32[16,32,128]{2,1,0:T(8,128)} %bitcast.30), channel_id=1, replica_groups=mesh['rows'=32,'cols'=16] {'cols'}, dimensions={0} | all-to-all | bytes 524288 | tf_op jit(solution)/shard_map/all_to_all | solution.py:41
  211.6 1.0 reduce_sum.107
  213.3 5.3 %all-to-all-start.7 = ((f32[16,32,128]{2,1,0:T(8,128)}), f32[16,32,128]{2,1,0:T(8,128)}, u32[]{:S(2)}, u32[]{:S(2)}) async-start(f32[16,32,128]{2,1,0:T(8,128)} %broadcast_in_dim.13), calls=%async_computation.7 | async-start | bytes 524288 | tf_op jit(solution)/shard_map/all_to_all | solution.py:24
  218.6 1.0 reshape.70
  219.9 0.8 fusion.5
  220.7 17.2 %all-to-all-done.7 = f32[16,32,128]{2,1,0:T(8,128)} async-done(((f32[16,32,128]{2,1,0:T(8,128)}), f32[16,32,128]{2,1,0:T(8,128)}, u32[]{:S(2)}, u32[]{:S(2)}) %all-to-all-start.7) | async-done | bytes 262176 | tf_op jit(solution)/shard_map/all_to_all | solution.py:24
  237.9 1.9 multiply_reduce_fusion.2
  239.8 16.4 %all_to_all.62 = f32[32,1,128]{2,1,0:T(1,128)S(1)} all-to-all(f32[32,1,128]{2,1,0:T(1,128)S(1)} %broadcast_in_dim.14), channel_id=1, replica_groups=mesh['rows'=32,'cols'=16] {'rows'}, dimensions={0} | all-to-all | bytes 32768 | tf_op jit(solution)/shard_map/all_to_all | solution.py:24
  (21 shorter events, 3.8 us)
Async XLA Ops:
  0.6 1.8 copy-start
  6.7 36.5 %copy-start.1 = (f32[1024,256]{1,0:T(8,128)S(1)}, f32[1024,256]{1,0:T(8,128)}, u32[]{:S(2)}) copy-start(f32[1024,256]{1,0:T(8,128)} %param.7) | copy-start | bytes 3145732
  37.6 21.6 %all-to-all-start.1 = ((f32[32,1,4104]{2,1,0:T(1,128)}), f32[32,1,4104]{2,1,0:T(1,128)}, u32[]{:S(2)}, u32[]{:S(2)}) async-start(f32[32,1,4104]{2,1,0:T(1,128)} %broadcast_in_dim.10), calls=%async_computation.1 | async-start | bytes 1081344 | tf_op jit(solution)/shard_map/all_to_all | solution.py:24
  185.8 52.1 %copy-start.2 = (f32[512,128]{1,0:T(8,128)S(1)}, f32[512,128]{1,0:T(8,128)}, u32[]{:S(2)}) copy-start(f32[512,128]{1,0:T(8,128)} %param.11) | copy-start | bytes 786436
  213.3 24.5 %all-to-all-start.7 = ((f32[16,32,128]{2,1,0:T(8,128)}), f32[16,32,128]{2,1,0:T(8,128)}, u32[]{:S(2)}, u32[]{:S(2)}) async-start(f32[16,32,128]{2,1,0:T(8,128)} %broadcast_in_dim.13), calls=%async_computation.7 | async-start | bytes 524288 | tf_op jit(solution)/shard_map/all_to_all | solution.py:24
  239.8 17.8 %copy-start.3 = (f32[512,128]{1,0:T(8,128)}, f32[512,128]{1,0:T(8,128)S(1)}, u32[]{:S(2)}) copy-start(f32[512,128]{1,0:T(8,128)S(1)} %get-tuple-element.4) | copy-start | bytes 786436
where the time goes:
time: 259 us; the launch traced here: 258 us
  blocking collectives  174 us (67%)
  waiting for transfers between devices  28.4 us (11%)
  matrix products  18.8 us (7%)
  other arithmetic  16.1 us (6%)
  local copies, waits for them, and re-layouts  10.3 us (4%)
  starting transfers between devices  9.66 us (4%)
    all_to_all x4, blocking collectives, summed_on_arrival(): lax.all_to_all(parts, axis, split_axis=0, concat_axis=0, tiled=True)  115 us
    all_to_all x3, blocking collectives, from_everyone(): lax.all_to_all(jnp.broadcast_to(value[None], (devices, *value.shape)), ax...  58.5 us
    all_to_all x2, waiting for transfers between devices, from_everyone(): lax.all_to_all(jnp.broadcast_to(value[None], (devices, *value.shape)), ax...  28.4 us
    all_to_all x2, starting transfers between devices, from_everyone(): lax.all_to_all(jnp.broadcast_to(value[None], (devices, *value.shape)), ax...  9.66 us
  transfers between devices with their start and end apart: 2, of which 2 were waited for; matrix products, arithmetic and copies ran while one was open for 3% of the time, Pallas kernels for 0%

commit v1 on v0

v1 whole, which is shorter than its diff:
```python
import functools

import jax
import jax.numpy as jnp
from jax import lax
from jax.experimental import pallas as pl
from jax.experimental.pallas import tpu as pltpu
from jax.sharding import PartitionSpec as P

ridge_weight = 0.02
MESH = pl.DeviceIdType.MESH
F32, BF16 = jnp.float32, jnp.bfloat16
T = 128
Q = 128


def split(a):
    high = a.astype(BF16)
    return high, (a - high.astype(F32)).astype(BF16)


def paired(a):
    return jnp.concatenate(split(a), axis=1)


def product(high, low, pair):
    both = jnp.dot(high, pair, preferred_element_type=F32) + jnp.dot(low, pair, preferred_element_type=F32)
    return both[:, :T] + both[:, T:]


def across(a, b, precision=lax.Precision.HIGHEST):
    return lax.dot_general(a, b, (((1,), (1,)), ((), ())), precision=precision, preferred_element_type=F32)


def rows_of(start, size):
    return pl.ds(pl.multiple_of(start, size), size)


def kernel(
    points, centers, factor, solution_, residual, direction,
    out_solution, out_residual, out_direction,
    away, own, core_in, y_in, z_in, full_c,
    part, x_in, zh_out, zh_in1, zh_in2, full_r,
    kh, kl, kth, ktl, rth, rtl,
    sm_out, sm_a, sm_z, sm_x,
    send, recv, send_s, recv_s,
):
    r, c = lax.axis_index("rows"), lax.axis_index("cols")
    y, zl, k = r // 8, (r // 2) % 4, r % 2
    x, zh = c // 4, c % 4

    def at(y_=None, zl_=None, k_=None, x_=None, zh_=None):
        pick = lambda new, old: old if new is None else new
        return (pick(y_, y) * 8 + pick(zl_, zl) * 2 + pick(k_, k), pick(x_, x) * 4 + pick(zh_, zh))

    sibling = at(k_=1 - k)
    ys = [at(y_=(y + j) % 4) for j in (1, 2, 3)]
    zls = [at(zl_=(zl + j) % 4) for j in (1, 2, 3)]
    xs = [at(x_=(x + j) % 4) for j in (1, 2, 3)]
    zh_a = at(zh_=zh + 1 - 2 * (zh % 2))
    zh_b = at(zh_=(zh + 3 - 2 * (zh % 2)) % 4)
    yk = y * 2 + k
    others = [(yk + j) % 8 for j in range(1, 8)]
    y_others = [at(y_=o // 2, k_=o % 2) for o in others]

    peers = zls + xs + [zh_a, zh_b] + y_others
    barrier = pltpu.get_barrier_semaphore()
    for p in peers:
        pl.semaphore_signal(barrier, inc=1, device_id=p, device_id_type=MESH)

    pending = []

    def copy(src, dst, s, d, device):
        return pltpu.make_async_remote_copy(
            src_ref=src, dst_ref=dst, send_sem=s, recv_sem=d, device_id=device, device_id_type=MESH
        )

    def push(src, dst, s, d, device):
        cp = copy(src, dst, s, d, device)
        cp.start()
        pending.append(cp)

    def arrived(dst, s, d):
        copy(dst, dst, s, d, sibling).wait_recv()

    def small_start(n, value):
        sm_a[n, yk] = value
        sm_out[n] = value
        for j, o in enumerate(y_others):
            push(sm_out.at[n], sm_a.at[n, yk], send_s.at[n, j], recv_s.at[n, yk], o)

    def small_middle(n):
        for j in range(7):
            arrived(sm_a.at[n, others[j]], send_s.at[n, j], recv_s.at[n, others[j]])
        total = sm_a[n, 0]
        for j in range(1, 8):
            total = total + sm_a[n, j]
        sm_z[n, zl] = total
        for j, o in enumerate(zls):
            push(sm_z.at[n, zl], sm_z.at[n, zl], send_s.at[n, 8 + j], recv_s.at[n, 8 + zl], o)

    def small_end(n):
        for j in (1, 2, 3):
            o = (zl + j) % 4
            arrived(sm_z.at[n, o], send_s.at[n, 8 + j - 1], recv_s.at[n, 8 + o])
        return (sm_z[n, 0] + sm_z[n, 1]) + (sm_z[n, 2] + sm_z[n, 3])

    def sum_over_rows(n, piece, ready, gaps):
        for q in range(4):
            away[n, q * Q : (q + 1) * Q] = piece((1 - k) * 512 + q * Q)
        ready()
        for q in range(4):
            rows = pl.ds(q * Q, Q)
            push(away.at[n, rows], core_in.at[n, rows], send.at[n, q], recv.at[n, q], sibling)
        for q in range(4):
            own[n, q * Q : (q + 1) * Q] = piece(k * 512 + q * Q)
        for j in (2, 1, 3, 0):
            q = (y + j) % 4
            rows = rows_of(q * Q, Q)
            arrived(core_in.at[n, rows], send.at[n, q], recv.at[n, q])
            own[n, rows] = own[n, rows] + core_in[n, rows]
            if j:
                push(own.at[n, rows], y_in.at[n, j - 1], send.at[n, 4 + j - 1], recv.at[n, 4 + j - 1], ys[j - 1])
        gaps[0]()
        mine = rows_of(y * Q, Q)
        for j in (1, 2, 3):
            arrived(y_in.at[n, j - 1], send.at[n, 4 + j - 1], recv.at[n, 4 + j - 1])
        z_in[n, zl] = (own[n, mine] + y_in[n, 0]) + (y_in[n, 1] + y_in[n, 2])
        for j in (3, 2, 1):
            push(z_in.at[n, zl], z_in.at[n, zl], send.at[n, 7 + j - 1], recv.at[n, 7 + zl], zls[j - 1])
        gaps[1]()
        for j in (1, 2, 3):
            o = (zl + j) % 4
            arrived(z_in.at[n, o], send.at[n, 7 + j - 1], recv.at[n, 7 + o])
        here = rows_of(k * 512 + y * Q, Q)
        full_c[n, here] = (z_in[n, 0] + z_in[n, 1]) + (z_in[n, 2] + z_in[n, 3])
        for j in (2, 1, 3):
            push(full_c.at[n, here], full_c.at[n, here], send.at[n, 11 + j - 1], recv.at[n, 11 + y], ys[j - 1])
        push(full_c.at[n, here], full_c.at[n, here], send.at[n, 15 + y], recv.at[n, 15 + y], sibling)
        gaps[2]()
        for j in (1, 3, 2):
            o = (y + j) % 4
            there = rows_of(k * 512 + o * Q, Q)
            arrived(full_c.at[n, there], send.at[n, 11 + j - 1], recv.at[n, 11 + o])
            push(full_c.at[n, there], full_c.at[n, there], send.at[n, 15 + o], recv.at[n, 15 + o], sibling)

    def sum_over_cols(n, high, low, gaps):
        mine, his = rows_of(k * 512, 512), rows_of((1 - k) * 512, 512)
        pair = paired(full_c[n, mine])
        for q in range(4):
            rows = pl.ds(q * Q, Q)
            part[n, rows] = product(high[rows, mine], low[rows, mine], pair)
        for o in range(4):
            there = rows_of((1 - k) * 512 + o * Q, Q)
            arrived(full_c.at[n, there], send.at[n, 15 + o], recv.at[n, 15 + o])
        pair = paired(full_c[n, his])
        for j in (2, 1, 3, 0):
            rows = rows_of((x + j) % 4 * Q, Q)
            part[n, rows] = part[n, rows] + product(high[rows, his], low[rows, his], pair)
            if j:
                push(part.at[n, rows], x_in.at[n, j - 1], send.at[n, 19 + j - 1], recv.at[n, 19 + j - 1], xs[j - 1])
        gaps[0]()
        here = rows_of(x * Q, Q)
        for j in (1, 2, 3):
            arrived(x_in.at[n, j - 1], send.at[n, 19 + j - 1], recv.at[n, 19 + j - 1])
        zh_out[n, 0] = (part[n, here] + x_in[n, 0]) + (x_in[n, 1] + x_in[n, 2])
        low_half, high_half = pl.ds(0, Q // 2), pl.ds(Q // 2, Q // 2)
        push(zh_out.at[n, 0, low_half], zh_in1.at[n, 0], send.at[n, 22], recv.at[n, 22], zh_a)
        push(zh_out.at[n, 0, high_half], zh_in1.at[n, 1], send.at[n, 23], recv.at[n, 23], zh_b)
        gaps[1]()
        arrived(zh_in1.at[n, 0], send.at[n, 22], recv.at[n, 22])
        zh_out[n, 1, low_half] = zh_out[n, 0, low_half] + zh_in1[n, 0]
        push(zh_out.at[n, 1, low_half], zh_in2.at[n, 0], send.at[n, 24], recv.at[n, 24], zh_b)
        arrived(zh_in1.at[n, 1], send.at[n, 23], recv.at[n, 23])
        zh_out[n, 1, high_half] = zh_out[n, 0, high_half] + zh_in1[n, 1]
        push(zh_out.at[n, 1, high_half], zh_in2.at[n, 1], send.at[n, 25], recv.at[n, 25], zh_a)
        gaps[2]()
        for half in (0, 1):
            arrived(zh_in2.at[n, half], send.at[n, 24 + half], recv.at[n, 24 + half])
        full_r[n, here] = zh_out[n, 1] + zh_in2[n].reshape(Q, T)
        for j in (2, 1, 3):
            push(full_r.at[n, here], full_r.at[n, here], send.at[n, 26 + j - 1], recv.at[n, 26 + x], xs[j - 1])
        gaps[3]()
        for j in (1, 3, 2):
            o = (x + j) % 4
            there = rows_of(o * Q, Q)
            arrived(full_r.at[n, there], send.at[n, 26 + j - 1], recv.at[n, 26 + o])

    def norms(a):
        return jnp.broadcast_to(jnp.sum(a * a, axis=0, keepdims=True), (8, T))

    def nothing():
        pass

    def kernel_rows(q, left, right, high, low):
        rows = pl.ds(q * Q, Q)
        a, b = left[rows, :], right[...]
        a_sq = jnp.sum(a * a, axis=1, keepdims=True)
        b_sq = across(jnp.ones((8, b.shape[1]), F32), b * b)[0:1]
        inner = across(a, b)
        high[rows, :], low[rows, :] = split(jnp.exp(-0.5 * ((a_sq + b_sq) - 2.0 * inner)))

    def some_kernel(which):
        def run():
            for q in which:
                kernel_rows(q, points, centers, kh, kl)

        return run

    def some_transposed(which):
        def run():
            for q in which:
                kernel_rows(q, centers, points, kth, ktl)

        return run

    def some_factor(which):
        def run():
            for q in which:
                rows = pl.ds(q * 256, 256)
                rth[:, q * 256 : (q + 1) * 256], rtl[:, q * 256 : (q + 1) * 256] = split(factor[rows, :].T)

        return run

    direction_pair = paired(direction[...])

    def mapped_piece(start):
        high, low = split(factor[rows_of(start, Q), :])
        return product(high, low, direction_pair)

    def entered():
        pl.semaphore_wait(barrier, len(peers))

    sum_over_rows(0, mapped_piece, entered, [some_kernel([0]), some_kernel([1, 2]), some_kernel([3])])
    sum_over_cols(
        0, kh, kl, [some_transposed([0]), some_transposed([1, 2, 3]), some_transposed([4, 5, 6]), some_transposed([7])]
    )

    predicted = full_r[0]
    predicted_pair = paired(predicted)
    lines = jnp.concatenate(
        [norms(residual[...])[0:1], norms(direction[...])[0:1], norms(predicted)[0:1], jnp.zeros((5, T), F32)], axis=0
    )

    def back_piece(start):
        rows = rows_of(start, Q)
        return product(kth[rows, :], ktl[rows, :], predicted_pair)

    def first_norms():
        some_factor([0])()
        small_start(0, lines)

    def second_norms():
        some_factor([1, 2])()
        small_middle(0)

    sum_over_rows(1, back_piece, nothing, [first_norms, second_norms, some_factor([3])])
    sum_over_cols(1, rth, rtl, [nothing] * 4)

    sums = small_end(0)
    norm_now = sums[0:1]
    step_size = norm_now / (sums[2:3] + ridge_weight * sums[1:2])
    old = direction[...]
    out_solution[...] = solution_[...] + step_size * old
    new_residual = residual[...] - step_size * (full_r[1] + ridge_weight * old)
    out_residual[...] = new_residual
    small_start(1, norms(new_residual))
    small_middle(1)
    norm_next = small_end(1)[0:1]
    out_direction[...] = new_residual + (norm_next / norm_now) * old
    for cp in pending:
        cp.wait_send()


def body(points, centers, factor, solution_, residual, direction):
    vmem = pl.BlockSpec(memory_space=pltpu.VMEM)
    out = jax.ShapeDtypeStruct(solution_.shape, F32)
    dma = pltpu.SemaphoreType.DMA
    v = lambda *shape: pltpu.VMEM(shape, F32)
    h = lambda *shape: pltpu.VMEM(shape, BF16)
    return pl.pallas_call(
        kernel,
        name="cg_iteration",
        out_shape=(out, out, out),
        in_specs=[vmem] * 6,
        out_specs=(vmem,) * 3,
        scratch_shapes=[
            v(2, 512, T), v(2, 512, T), v(2, 512, T), v(2, 3, Q, T), v(2, 4, Q, T), v(2, 1024, T),
            v(2, 512, T), v(2, 3, Q, T), v(2, 2, Q, T), v(2, 2, Q // 2, T), v(2, 2, Q // 2, T), v(2, 512, T),
            h(512, 1024), h(512, 1024), h(1024, 512), h(1024, 512), h(512, 1024), h(512, 1024),
            v(2, 8, T), v(2, 8, 8, T), v(2, 4, 8, T), v(2, 4, 8, T),
            dma((2, 32)), dma((2, 32)), dma((2, 16)), dma((2, 16)),
        ],
        compiler_params=pltpu.CompilerParams(collective_id=0, has_side_effects=True, vmem_limit_bytes=60 * 2**20),
    )(points, centers, factor, solution_, residual, direction)


def solution(mesh):
    return jax.shard_map(
        body,
        mesh=mesh,
        in_specs=(
            P("rows", None),
            P("cols", None),
            P("cols", "rows"),
            P("rows", None),
            P("rows", None),
            P("rows", None),
        ),
        out_specs=(P("rows", None), P("rows", None), P("rows", None)),
        check_vma=False,
    )
```

time: 259 us -> 114 us (0.44)
  blocking collectives: 174 us -> 0 us
  Pallas kernels: 0 us -> 108 us
  waiting for transfers between devices: 28.4 us -> 0 us
  matrix products: 18.8 us -> 0 us
  other arithmetic: 16.1 us -> 0 us
  starting transfers between devices: 9.66 us -> 0 us
  local copies, waits for them, and re-layouts: 10.3 us -> 5.01 us
    all_to_all x7 -> x0, blocking collectives: 174 us -> none  [the longest x4 115 us: summed_on_arrival(): lax.all_to_all(parts, axis, split_axis=0, concat_axis=0, tiled=True)]
    pallas_call x0 -> x1, Pallas kernels: none -> 108 us  [body(): pl.pallas_call(kernel, name='cg_iteration', out_shape=(out, out, out), in...]
    all_to_all x2 -> x0, waiting for transfers between devices: 28.4 us -> none  [from_everyone(): lax.all_to_all(jnp.broadcast_to(value[None], (devices, *value.shape)), ax...]
    dot_general x5 -> x0, matrix products: 18.8 us -> none  [the longest x1 5.01 us: body(): lax.dot_general(kernel, predicted, (((0,), (0,)), ((), ())), precision=hi...]
    all_to_all x2 -> x0, starting transfers between devices: 9.66 us -> none  [from_everyone(): lax.all_to_all(jnp.broadcast_to(value[None], (devices, *value.shape)), ax...]
    reduce_sum x10 -> x0, other arithmetic: 8.37 us -> none  [the longest x4 3.73 us: summed_on_arrival(): return arrived.sum(axis=0)]
    all_to_all x2 -> x0, other arithmetic: 4.67 us -> none  [from_everyone(): lax.all_to_all(jnp.broadcast_to(value[None], (devices, *value.shape)), ax...]
    unnamed x8 -> x3, local copies, waits for them, and re-layouts: 0.5 us -> 5.01 us
  transfers between devices with their start and end apart: 2 -> 0, of which waited for: 2 -> 0; matrix products, arithmetic and copies ran while one was open for 3% -> 0% of each run, Pallas kernels for 0% -> 0%
where the time goes in v1:
time: 114 us
  Pallas kernels  108 us (95%)
  local copies, waits for them, and re-layouts  5.01 us (4%)
    pallas_call x1, Pallas kernels, body(): pl.pallas_call(kernel, name='cg_iteration', out_shape=(out, out, out), in...  108 us
    unnamed x3, local copies, waits for them, and re-layouts  5.01 us

profile of v1, /device:TPU:1, one launch (start us, length us, event | category | flops | bytes accessed | tf_op | source)
XLA Modules:
  0.0 113.8 jit_solution(3534567388734170471)
XLA Ops:
  0.6 108.1 %cg_iteration.1 = (f32[512,128]{1,0:T(8,128)}, f32[512,128]{1,0:T(8,128)}, f32[512,128]{1,0:T(8,128)}) custom-call(f32[512,256]{1,0:T(8,128)} %points.1, f32[1024,256]{1,0:T(8,128)} %centers.1, f32[1024,512]{1,0:T(8,128)} %factor.1, f32[512,128]{1,0:T(8,128)} %solution_.1, f32[512,128]{1,0:T(8,128)} %residual.1, f32[512,128]{1,0:T(8,128)} %direction.1), custom_call_target="tpu_custom_call" | custom-call | tf_op jit(solution)/shard_map/cg_iteration/pallas_call | solution.py:281
  108.8 1.7 %copy.12 = f32[512,128]{1,0:T(8,128)} copy(f32[512,128]{1,0:T(8,128)} %get-tuple-element.6) | data formatting | bytes 524288
  110.5 1.7 %copy.13 = f32[512,128]{1,0:T(8,128)} copy(f32[512,128]{1,0:T(8,128)} %get-tuple-element.7) | data formatting | bytes 524288
  112.1 1.7 %copy.14 = f32[512,128]{1,0:T(8,128)} copy(f32[512,128]{1,0:T(8,128)} %get-tuple-element.8) | data formatting | bytes 524288

commit v2 on v0

v2 whole, which is shorter than its diff:
```python
import jax
import jax.numpy as jnp
from jax import lax
from jax.experimental import pallas as pl
from jax.experimental.pallas import tpu as pltpu
from jax.sharding import PartitionSpec as P

ridge_weight = 0.02
MESH = pl.DeviceIdType.MESH
F32, BF16 = jnp.float32, jnp.bfloat16
T = 128
W = 64
Q = 128
H = 64


def split(a):
    high = a.astype(BF16)
    return high, (a - high.astype(F32)).astype(BF16)


def swap(a):
    return pltpu.roll(a, W, 1)


def first_lanes(rows):
    return lax.broadcasted_iota(jnp.int32, (rows, T), 1) < W


def pack(full, chain):
    top, bottom = full[:H], full[H:]
    if chain == 0:
        return jnp.where(first_lanes(H), top, swap(bottom))
    return jnp.where(first_lanes(H), swap(top), bottom)


def unpack(a, b):
    m = first_lanes(H)
    return jnp.concatenate([jnp.where(m, a, swap(b)), jnp.where(m, swap(a), b)], axis=0)


def fold(both):
    total = both + swap(both)
    return jnp.where(first_lanes(H), total[:H], total[H:])


def operand(packed):
    high = packed.astype(BF16).astype(F32)
    low = packed - high
    m = first_lanes(H)
    return jnp.concatenate([jnp.where(m, high, swap(low)), jnp.where(m, swap(high), low)], axis=0).astype(BF16)


def dot(a, b):
    return jnp.dot(a, b, preferred_element_type=F32)


def across(a, b):
    return lax.dot_general(
        a, b, (((1,), (1,)), ((), ())), precision=lax.Precision.HIGHEST, preferred_element_type=F32
    )


def rows_of(start, size):
    return pl.ds(pl.multiple_of(start, size), size)


def kernel(
    points_, centers_, factor_, residual_, direction_,
    image_, step_out, ratio_out,
    points, centers, factor, residual, direction, image,
    away, own, core_in, y_in, z_in, full_c,
    part, x_in, zh_out, zh_in1, zh_in2, full_r,
    kh, kl, kth, ktl, rth, rtl,
    sm_out, sm_a, sm_b,
    send, recv, send_s, recv_s, local,
):
    r, c = lax.axis_index("rows"), lax.axis_index("cols")
    y, zl, k = r // 8, (r // 2) % 4, r % 2
    x, zh = c // 4, c % 4

    def at(y_=None, zl_=None, k_=None, x_=None, zh_=None):
        pick = lambda new, old: old if new is None else new
        return (pick(y_, y) * 8 + pick(zl_, zl) * 2 + pick(k_, k), pick(x_, x) * 4 + pick(zh_, zh))

    sibling = at(k_=1 - k)
    ys = [at(y_=(y + j) % 4) for j in (1, 2, 3)]
    zls = [at(zl_=(zl + j) % 4) for j in (1, 2, 3)]
    xs = [at(x_=(x + j) % 4) for j in (1, 2, 3)]
    zh_a = at(zh_=zh + 1 - 2 * (zh % 2))
    zh_b = at(zh_=(zh + 3 - 2 * (zh % 2)) % 4)
    xk, yz = x * 2 + k, y * 4 + zl
    other_xk = [(x + j) % 4 * 2 + (k + e) % 2 for j in range(4) for e in range(2)][1:]
    other_yz = [(y + j) % 4 * 4 + (zl + e) % 4 for j in range(4) for e in range(4)][1:]
    xks = [at(x_=o // 2, k_=o % 2) for o in other_xk]
    yzs = [at(y_=o // 4, zl_=o % 4) for o in other_yz]

    peers = [zh_a, zh_b] + yzs + xks
    barrier = pltpu.get_barrier_semaphore()
    for p in peers:
        pl.semaphore_signal(barrier, inc=1, device_id=p, device_id_type=MESH)

    here_half, there_half = rows_of(k * 512, 512), rows_of((1 - k) * 512, 512)
    loads = [
        pltpu.make_async_copy(a, b, local.at[i])
        for i, (a, b) in enumerate(
            [
                (direction_, direction),
                (factor_.at[there_half], factor.at[there_half]),
                (factor_.at[here_half], factor.at[here_half]),
                (centers_, centers),
                (points_, points),
                (residual_, residual),
            ]
        )
    ]
    for load in loads:
        load.start()

    pending = []

    def copy(src, dst, s, d, device):
        return pltpu.make_async_remote_copy(
            src_ref=src, dst_ref=dst, send_sem=s, recv_sem=d, device_id=device, device_id_type=MESH
        )

    def push(src, dst, s, d, device):
        cp = copy(src, dst, s, d, device)
        cp.start()
        pending.append(cp)

    def arrived(dst, s, d):
        copy(dst, dst, s, d, sibling).wait_recv()

    def small_start(n, value, slot, slots, devices):
        sm_a[n, slot] = value
        sm_out[n] = value
        for j, device in enumerate(devices):
            push(sm_out.at[n], sm_a.at[n, slot], send_s.at[n, j], recv_s.at[n, slot], device)

    def small_middle(n, slots, count):
        for j, o in enumerate(slots):
            arrived(sm_a.at[n, o], send_s.at[n, j], recv_s.at[n, o])
        total = sm_a[n, 0]
        for j in range(1, count):
            total = total + sm_a[n, j]
        sm_b[n, yz] = total
        for j, device in enumerate(yzs):
            push(sm_b.at[n, yz], sm_b.at[n, yz], send_s.at[n, 8 + j], recv_s.at[n, 8 + yz], device)

    def small_end(n):
        for j, o in enumerate(other_yz):
            arrived(sm_b.at[n, o], send_s.at[n, 8 + j], recv_s.at[n, 8 + o])
        total = sm_b[n, 0]
        for j in range(1, 16):
            total = total + sm_b[n, j]
        return total

    def send_away(s):
        for q in range(4):
            rows = pl.ds(q * H, H)
            push(away.at[s, rows], core_in.at[s, rows], send.at[s, q], recv.at[s, q], sibling)

    def chain(p, n, high, low):
        s = 2 * n + p
        yield
        for j in (2, 1, 3, 0):
            q = (y + j) % 4
            rows = rows_of(q * H, H)
            arrived(core_in.at[s, rows], send.at[s, q], recv.at[s, q])
            own[s, rows] = own[s, rows] + core_in[s, rows]
            if j:
                push(own.at[s, rows], y_in.at[s, j - 1], send.at[s, 4 + j - 1], recv.at[s, 4 + j - 1], ys[j - 1])
        yield
        mine = rows_of(y * H, H)
        for j in (1, 3, 2):
            arrived(y_in.at[s, j - 1], send.at[s, 4 + j - 1], recv.at[s, 4 + j - 1])
        z_in[s, zl] = (own[s, mine] + y_in[s, 0]) + (y_in[s, 1] + y_in[s, 2])
        for j in (2, 1, 3):
            push(z_in.at[s, zl], z_in.at[s, zl], send.at[s, 7 + j - 1], recv.at[s, 7 + zl], zls[j - 1])
        yield
        for j in (1, 3, 2):
            o = (zl + j) % 4
            arrived(z_in.at[s, o], send.at[s, 7 + j - 1], recv.at[s, 7 + o])
        here = rows_of(k * 256 + y * H, H)
        full_c[s, here] = (z_in[s, 0] + z_in[s, 1]) + (z_in[s, 2] + z_in[s, 3])
        for j in (2, 1, 3):
            push(full_c.at[s, here], full_c.at[s, here], send.at[s, 11 + j - 1], recv.at[s, 11 + y], ys[j - 1])
        push(full_c.at[s, here], full_c.at[s, here], send.at[s, 15 + y], recv.at[s, 15 + y], sibling)
        yield
        for j in (1, 3, 2):
            o = (y + j) % 4
            there = rows_of(k * 256 + o * H, H)
            arrived(full_c.at[s, there], send.at[s, 11 + j - 1], recv.at[s, 11 + o])
            push(full_c.at[s, there], full_c.at[s, there], send.at[s, 15 + o], recv.at[s, 15 + o], sibling)
        mine, his = rows_of(k * 512, 512), rows_of((1 - k) * 512, 512)

        def half(base):
            return jnp.concatenate([operand(full_c[s, rows_of(base * 256 + q * H, H)]) for q in range(4)], axis=0)

        b = half(k)
        for q in range(4):
            rows = pl.ds(q * Q, Q)
            part[s, rows] = dot(high[rows, mine], b) + dot(low[rows, mine], b)
        yield
        for o in range(4):
            there = rows_of((1 - k) * 256 + o * H, H)
            arrived(full_c.at[s, there], send.at[s, 15 + o], recv.at[s, 15 + o])
        b = half(1 - k)
        for j in (2, 1, 3, 0):
            q = (x + j) % 4
            rows = rows_of(q * Q, Q)
            slot = zh_out.at[s, 0] if j == 0 else zh_out.at[s, 1 + j]
            slot[...] = fold(part[s, rows] + (dot(high[rows, his], b) + dot(low[rows, his], b)))
            if j:
                push(slot, x_in.at[s, j - 1], send.at[s, 19 + j - 1], recv.at[s, 19 + j - 1], xs[j - 1])
        yield
        for j in (1, 3, 2):
            arrived(x_in.at[s, j - 1], send.at[s, 19 + j - 1], recv.at[s, 19 + j - 1])
        zh_out[s, 0] = (zh_out[s, 0] + x_in[s, 0]) + (x_in[s, 1] + x_in[s, 2])
        first, second = pl.ds(0, H // 2), pl.ds(H // 2, H // 2)
        push(zh_out.at[s, 0, first], zh_in1.at[s, 0], send.at[s, 22], recv.at[s, 22], zh_a)
        push(zh_out.at[s, 0, second], zh_in1.at[s, 1], send.at[s, 23], recv.at[s, 23], zh_b)
        yield
        arrived(zh_in1.at[s, 0], send.at[s, 22], recv.at[s, 22])
        zh_out[s, 1, first] = zh_out[s, 0, first] + zh_in1[s, 0]
        push(zh_out.at[s, 1, first], zh_in2.at[s, 0], send.at[s, 24], recv.at[s, 24], zh_b)
        arrived(zh_in1.at[s, 1], send.at[s, 23], recv.at[s, 23])
        zh_out[s, 1, second] = zh_out[s, 0, second] + zh_in1[s, 1]
        push(zh_out.at[s, 1, second], zh_in2.at[s, 1], send.at[s, 25], recv.at[s, 25], zh_a)
        yield
        here = rows_of(x * H, H)
        for e in (0, 1):
            arrived(zh_in2.at[s, e], send.at[s, 24 + e], recv.at[s, 24 + e])
        full_r[s, here] = zh_out[s, 1] + zh_in2[s].reshape(H, T)
        for j in (2, 1, 3):
            push(full_r.at[s, here], full_r.at[s, here], send.at[s, 26 + j - 1], recv.at[s, 26 + x], xs[j - 1])
        yield
        for j in (1, 3, 2):
            o = (x + j) % 4
            there = rows_of(o * H, H)
            arrived(full_r.at[s, there], send.at[s, 26 + j - 1], recv.at[s, 26 + o])

    def back_terms(p):
        s = 2 + p
        b = jnp.concatenate([operand(full_r[p, q * H : (q + 1) * H]) for q in range(4)], axis=0)
        for q in range(4):
            rows = rows_of((1 - k) * 512 + q * Q, Q)
            away[s, q * H : (q + 1) * H] = fold(dot(kth[rows, :], b) + dot(ktl[rows, :], b))
        send_away(s)
        for q in range(4):
            rows = rows_of(k * 512 + q * Q, Q)
            own[s, q * H : (q + 1) * H] = fold(dot(kth[rows, :], b) + dot(ktl[rows, :], b))

    def whole(p):
        yield from chain(p, 0, kh, kl)
        back_terms(p)
        yield from chain(p, 1, rth, rtl)

    def kernel_block(e):
        def run():
            if e == 0:
                loads[3].wait()
                loads[4].wait()
            cols = slice(e * 256, (e + 1) * 256)
            a, b = points[...], centers[cols, :]
            a_sq = jnp.sum(a * a, axis=1, keepdims=True)
            b_sq = across(jnp.ones((8, b.shape[1]), F32), b * b)[0:1]
            block = jnp.exp(-0.5 * ((a_sq + b_sq) - 2.0 * across(a, b)))
            kh[:, cols], kl[:, cols] = split(block)
            kth[cols, :], ktl[cols, :] = split(block.T)

        return run

    def factor_block(e):
        def run():
            cols = slice(e * 256, (e + 1) * 256)
            rth[:, cols], rtl[:, cols] = split(factor[cols, :].T)

        return run

    def norm(a):
        return jnp.sum(a * a, axis=0, keepdims=True)

    def first_norms():
        loads[5].wait()
        squares = [norm(full_r[p]) for p in (0, 1)]
        squares = [a + swap(a) for a in squares]
        predicted = jnp.where(first_lanes(1), squares[0], squares[1])
        lines = [norm(residual[...]), norm(direction[...]), predicted, jnp.zeros((5, T), F32)]
        small_start(0, jnp.concatenate(lines, axis=0), k, [1 - k], [sibling])

    def second_norms():
        small_middle(0, [1 - k], 2)

    loads[0].wait()
    pair = jnp.concatenate(split(direction[...]), axis=1)

    def mapped(base, target):
        for q in range(4):
            high, low = split(factor[rows_of(base * 512 + q * Q, Q), :])
            both = dot(high, pair) + dot(low, pair)
            both = both[:, :T] + both[:, T:]
            for p in (0, 1):
                target[p, q * H : (q + 1) * H] = pack(both, p)

    loads[1].wait()
    mapped(1 - k, away)
    pl.semaphore_wait(barrier, len(peers))
    for p in (0, 1):
        send_away(p)
    loads[2].wait()
    mapped(k, own)

    chains = [whole(0), whole(1)]
    extra = {
        1: [kernel_block(0)],
        2: [kernel_block(1), kernel_block(2)],
        3: [kernel_block(3)],
        6: [factor_block(0), factor_block(1)],
        7: [factor_block(2), factor_block(3)],
        10: [first_norms],
        12: [second_norms],
    }
    for step in range(18):
        for p in (0, 1):
            next(chains[p])
        for run in extra.get(step, []):
            run()

    sums = small_end(0)
    norm_now = sums[0:1]
    step_size = norm_now / (sums[2:3] + ridge_weight * sums[1:2])
    quarter = rows_of(x * Q, Q)
    packed = rows_of(x * H, H)
    fresh = residual[quarter, :] - step_size * (
        unpack(full_r[2, packed], full_r[3, packed]) + ridge_weight * direction[quarter, :]
    )
    small_start(1, jnp.broadcast_to(norm(fresh), (8, T)), xk, other_xk, xks)
    for p in (0, 1):
        for unused in chains[p]:
            pass
    for q in range(4):
        rows = pl.ds(q * H, H)
        image[q * Q : (q + 1) * Q] = unpack(full_r[2, rows], full_r[3, rows])
    out = pltpu.make_async_copy(image, image_, local.at[6])
    out.start()
    small_middle(1, other_xk, 8)
    norm_next = small_end(1)[0:1]
    step_out[...] = step_size
    ratio_out[...] = norm_next / norm_now
    for cp in pending:
        cp.wait_send()
    out.wait()


def body(points, centers, factor, solution_, residual, direction):
    vmem, anywhere = pl.BlockSpec(memory_space=pltpu.VMEM), pl.BlockSpec(memory_space=pl.ANY)
    dma = pltpu.SemaphoreType.DMA
    v = lambda *shape: pltpu.VMEM(shape, F32)
    h = lambda *shape: pltpu.VMEM(shape, BF16)
    image, step_size, ratio = pl.pallas_call(
        kernel,
        name="cg_iteration",
        out_shape=(jax.ShapeDtypeStruct(direction.shape, F32), jax.ShapeDtypeStruct((1, T), F32), jax.ShapeDtypeStruct((1, T), F32)),
        in_specs=[anywhere] * 5,
        out_specs=(anywhere, vmem, vmem),
        scratch_shapes=[
            v(512, 256), v(1024, 256), v(1024, 512), v(512, T), v(512, T), v(512, T),
            v(4, 256, T), v(4, 256, T), v(4, 256, T), v(4, 3, H, T), v(4, 4, H, T), v(4, 512, T),
            v(4, 512, T), v(4, 3, H, T), v(4, 5, H, T), v(4, 2, H // 2, T), v(4, 2, H // 2, T), v(4, 256, T),
            h(512, 1024), h(512, 1024), h(1024, 512), h(1024, 512), h(512, 1024), h(512, 1024),
            v(2, 8, T), v(2, 8, 8, T), v(2, 16, 8, T),
            dma((4, 32)), dma((4, 32)), dma((2, 24)), dma((2, 24)), dma((8,)),
        ],
        compiler_params=pltpu.CompilerParams(collective_id=0, has_side_effects=True, vmem_limit_bytes=60 * 2**20),
    )(points, centers, factor, residual, direction)
    new_solution = solution_ + step_size * direction
    new_residual = residual - step_size * (image + ridge_weight * direction)
    return new_solution, new_residual, new_residual + ratio * direction


def solution(mesh):
    return jax.shard_map(
        body,
        mesh=mesh,
        in_specs=(
            P("rows", None),
            P("cols", None),
            P("cols", "rows"),
            P("rows", None),
            P("rows", None),
            P("rows", None),
        ),
        out_specs=(P("rows", None), P("rows", None), P("rows", None)),
        check_vma=False,
    )
```

time: 259 us -> 100 us (0.39)
  blocking collectives: 174 us -> 0 us
  Pallas kernels: 0 us -> 97.6 us
  waiting for transfers between devices: 28.4 us -> 0 us
  matrix products: 18.8 us -> 0 us
  other arithmetic: 16.1 us -> 1.89 us
  local copies, waits for them, and re-layouts: 10.3 us -> 0.01 us
  starting transfers between devices: 9.66 us -> 0 us
    all_to_all x7 -> x0, blocking collectives: 174 us -> none  [the longest x4 115 us: summed_on_arrival(): lax.all_to_all(parts, axis, split_axis=0, concat_axis=0, tiled=True)]
    pallas_call x0 -> x1, Pallas kernels: none -> 97.6 us  [body(): pl.pallas_call(kernel, name='cg_iteration', out_shape=(jax.ShapeDtypeStru...]
    all_to_all x2 -> x0, waiting for transfers between devices: 28.4 us -> none  [from_everyone(): lax.all_to_all(jnp.broadcast_to(value[None], (devices, *value.shape)), ax...]
    dot_general x5 -> x0, matrix products: 18.8 us -> none  [the longest x1 5.01 us: body(): lax.dot_general(kernel, predicted, (((0,), (0,)), ((), ())), precision=hi...]
    all_to_all x2 -> x0, starting transfers between devices: 9.66 us -> none  [from_everyone(): lax.all_to_all(jnp.broadcast_to(value[None], (devices, *value.shape)), ax...]
    reduce_sum x10 -> x0, other arithmetic: 8.37 us -> none  [the longest x4 3.73 us: summed_on_arrival(): return arrived.sum(axis=0)]
    all_to_all x2 -> x0, other arithmetic: 4.67 us -> none  [from_everyone(): lax.all_to_all(jnp.broadcast_to(value[None], (devices, *value.shape)), ax...]
    all_to_all x2 -> x0, local copies, waits for them, and re-layouts: 3.3 us -> none  [summed_on_arrival(): lax.all_to_all(parts, axis, split_axis=0, concat_axis=0, tiled=True)]
  transfers between devices with their start and end apart: 2 -> 0, of which waited for: 2 -> 0; matrix products, arithmetic and copies ran while one was open for 3% -> 0% of each run, Pallas kernels for 0% -> 0%
where the time goes in v2:
time: 100 us
  Pallas kernels  97.6 us (98%)
  other arithmetic  1.89 us (2%)
    pallas_call x1, Pallas kernels, body(): pl.pallas_call(kernel, name='cg_iteration', out_shape=(jax.ShapeDtypeStru...  97.6 us

profile of v2, /device:TPU:1, one launch (start us, length us, event | category | flops | bytes accessed | tf_op | source)
XLA Modules:
  0.0 100.2 jit_solution(5248808026292416314)
XLA Ops:
  0.6 0.0 copy-start
  0.6 0.0 copy-start.1
  0.7 0.0 copy-start.2
  0.7 97.6 %cg_iteration.1 = (f32[512,128]{1,0:T(8,128)}, f32[1,128]{1,0:T(1,128)}, f32[1,128]{1,0:T(1,128)}) custom-call(f32[512,256]{1,0:T(8,128)} %points_.1, f32[1024,256]{1,0:T(8,128)} %centers_.1, f32[1024,512]{1,0:T(8,128)} %factor_.1, f32[512,128]{1,0:T(8,128)} %residual_.1, f32[512,128]{1,0:T(8,128)} %direction_.1), custom_call_target="tpu_custom_call" | custom-call | tf_op jit(solution)/shard_map/cg_iteration/pallas_call | solution.py:362
  98.3 0.0 copy-done
  98.3 0.0 copy-done.1
  98.3 0.0 copy-done.2
  98.3 1.9 %multiply_add_fusion = (f32[512,128]{1,0:T(8,128)}, f32[512,128]{1,0:T(8,128)}, f32[512,128]{1,0:T(8,128)}) fusion(f32[512,128]{1,0:T(8,128)S(1)} %copy-done, f32[128]{0:T(128)} %bitcast.3, f32[512,128]{1,0:T(8,128)S(1)} %copy-done.1, f32[512,128]{1,0:T(8,128)} %get-tuple-element.7, f32[128]{0:T(128)} %bitcast.2, f32[512,128]{1,0:T(8,128)S(1)} %copy-done.2), kind=kLoop, calls=%fused_computation | loop fusion | flops 524288 | bytes 1836032 | tf_op jit(solution)/shard_map/add | solution.py:380
Async XLA Ops:
  0.6 97.7 %copy-start = (f32[512,128]{1,0:T(8,128)S(1)}, f32[512,128]{1,0:T(8,128)}, u32[]{:S(2)}) copy-start(f32[512,128]{1,0:T(8,128)} %direction_.1) | copy-start | bytes 786436
  0.6 97.7 %copy-start.1 = (f32[512,128]{1,0:T(8,128)S(1)}, f32[512,128]{1,0:T(8,128)}, u32[]{:S(2)}) copy-start(f32[512,128]{1,0:T(8,128)} %residual_.1) | copy-start | bytes 786436
  0.7 97.7 %copy-start.2 = (f32[512,128]{1,0:T(8,128)S(1)}, f32[512,128]{1,0:T(8,128)}, u32[]{:S(2)}) copy-start(f32[512,128]{1,0:T(8,128)} %param.9) | copy-start | bytes 786436

commit v3 on v2

v3 whole, which is shorter than its diff:
```python
import jax
import jax.numpy as jnp
from jax import lax
from jax.experimental import pallas as pl
from jax.experimental.pallas import tpu as pltpu
from jax.sharding import PartitionSpec as P

ridge_weight = 0.02
MESH = pl.DeviceIdType.MESH
F32, BF16 = jnp.float32, jnp.bfloat16
T = 128
W = 64
Q = 128
H = 64


def split(a):
    high = a.astype(BF16)
    return high, (a - high.astype(F32)).astype(BF16)


def swap(a):
    return pltpu.roll(a, W, 1)


def first_lanes(rows):
    return lax.broadcasted_iota(jnp.int32, (rows, T), 1) < W


def pack(full, chain):
    top, bottom = full[:H], full[H:]
    if chain == 0:
        return jnp.where(first_lanes(H), top, swap(bottom))
    return jnp.where(first_lanes(H), swap(top), bottom)


def unpack(a, b):
    m = first_lanes(H)
    return jnp.concatenate([jnp.where(m, a, swap(b)), jnp.where(m, swap(a), b)], axis=0)


def fold(both):
    total = both + swap(both)
    return jnp.where(first_lanes(H), total[:H], total[H:])


def operand(packed):
    high = packed.astype(BF16).astype(F32)
    low = packed - high
    m = first_lanes(H)
    return jnp.concatenate([jnp.where(m, high, swap(low)), jnp.where(m, swap(high), low)], axis=0).astype(BF16)


def dot(a, b):
    return jnp.dot(a, b, preferred_element_type=F32)


def across(a, b):
    return lax.dot_general(
        a, b, (((1,), (1,)), ((), ())), precision=lax.Precision.HIGHEST, preferred_element_type=F32
    )


def rows_of(start, size):
    return pl.ds(pl.multiple_of(start, size), size)


def kernel(
    points_, centers_, factor_, residual_, direction_,
    image_, step_out, ratio_out,
    points, centers, factor, residual, direction, image,
    away, own, core_in, a_in, b_in, full_c,
    part, x_in, zh_out, zh_in1, zh_in2, full_r,
    kh, kl, kth, ktl, rth, rtl,
    small_a, small_b, line,
    send, recv, small_send, small_recv, local,
):
    r, c = lax.axis_index("rows"), lax.axis_index("cols")
    y, zl, k = r // 8, (r // 2) % 4, r % 2
    x, zh = c // 4, c % 4

    def at(y_=None, zl_=None, k_=None, x_=None, zh_=None):
        pick = lambda new, old: old if new is None else new
        return (pick(y_, y) * 8 + pick(zl_, zl) * 2 + pick(k_, k), pick(x_, x) * 4 + pick(zh_, zh))

    sibling = at(k_=1 - k)
    ys = [at(y_=(y + j) % 4) for j in (1, 2, 3)]
    zls = [at(zl_=(zl + j) % 4) for j in (1, 2, 3)]
    xs = [at(x_=(x + j) % 4) for j in (1, 2, 3)]
    zh_a = at(zh_=zh + 1 - 2 * (zh % 2))
    zh_b = at(zh_=(zh + 3 - 2 * (zh % 2)) % 4)
    column = [at((y + i) % 4, (zl + j) % 4, (k + e) % 2) for i in (2, 1, 3, 0) for j in (2, 1, 3, 0) for e in (1, 0)][:-1]

    here_half, there_half = rows_of(k * 512, 512), rows_of((1 - k) * 512, 512)
    loads = [
        pltpu.make_async_copy(a, b, local.at[i])
        for i, (a, b) in enumerate(
            [
                (direction_, direction),
                (factor_.at[there_half], factor.at[there_half]),
                (factor_.at[here_half], factor.at[here_half]),
                (centers_, centers),
                (points_, points),
                (residual_, residual),
            ]
        )
    ]
    loads[0].start()
    loads[1].start()

    peers = [zh_a, zh_b] + column + xs
    barrier = pltpu.get_barrier_semaphore()
    for p in peers:
        pl.semaphore_signal(barrier, inc=1, device_id=p, device_id_type=MESH)

    for load in loads[2:]:
        load.start()

    def copy(src, dst, s, d, device):
        return pltpu.make_async_remote_copy(
            src_ref=src, dst_ref=dst, send_sem=s, recv_sem=d, device_id=device, device_id_type=MESH
        )

    small = [small_a, small_b]

    def push(src, dst, s, phase, d, device):
        copy(src, dst, send.at[s % 2, phase], recv.at[s, d], device).start()

    def arrived(like, s, d):
        copy(like, like, send.at[s % 2, 0], recv.at[s, d], sibling).wait_recv()

    def sent(s, phase):
        like = {0: away, 4: away, 6: zh_in1, 7: zh_in2}.get(phase, a_in).at[s]
        copy(like, like, send.at[s % 2, phase], recv.at[s, 0], sibling).wait_send()

    def small_start(n, value):
        lines = small[n]
        lines[r] = value
        for device in column:
            copy(lines.at[r], lines.at[r], small_send.at[n], small_recv.at[n], device).start()

    def small_end(n):
        like = small[n].at[pl.ds(0, 31)]
        copy(like, like, small_send.at[n], small_recv.at[n], sibling).wait()
        return jnp.sum(small[n][...], axis=0)

    def send_away(s):
        if s > 1:
            sent(s, 0)
        for q in range(4):
            rows = pl.ds(q * H, H)
            push(away.at[s, rows], core_in.at[s, rows], s, 0, q, sibling)

    def chain(p, n, high, low):
        s = 2 * n + p
        (a, a_devices), (b, b_devices) = [((y, ys), (zl, zls)), ((zl, zls), (y, ys))][p]

        def again(*phases):
            for phase in phases if n else ():
                sent(s, phase)

        yield
        again(1)
        for j in (2, 1, 3, 0):
            q = (a + j) % 4
            rows = rows_of(q * H, H)
            arrived(core_in.at[s, rows], s, q)
            own[s, rows] = own[s, rows] + core_in[s, rows]
            if j:
                push(own.at[s, rows], a_in.at[s, j - 1], s, 1, 4, a_devices[j - 1])
        again(2)
        yield
        mine = rows_of(a * H, H)
        arrived(a_in.at[s], s, 4)
        b_in[s, b] = (own[s, mine] + a_in[s, 0]) + (a_in[s, 1] + a_in[s, 2])
        for j in (2, 1, 3):
            push(b_in.at[s, b], b_in.at[s, b], s, 2, 5, b_devices[j - 1])
        again(3, 4)
        yield
        arrived(a_in.at[s], s, 5)
        here = rows_of(k * 256 + a * H, H)
        full_c[s, here] = (b_in[s, 0] + b_in[s, 1]) + (b_in[s, 2] + b_in[s, 3])
        for j in (2, 1, 3):
            push(full_c.at[s, here], full_c.at[s, here], s, 3, 6 + j - 1, a_devices[j - 1])
        push(full_c.at[s, here], full_c.at[s, here], s, 4, 9, sibling)
        yield
        for j in (1, 3, 2):
            there = rows_of(k * 256 + (a + 4 - j) % 4 * H, H)
            arrived(full_c.at[s, there], s, 6 + j - 1)
            push(full_c.at[s, there], full_c.at[s, there], s, 4, 9, sibling)
        mine, his = rows_of(k * 512, 512), rows_of((1 - k) * 512, 512)

        def half(base):
            return jnp.concatenate([operand(full_c[s, rows_of(base * 256 + q * H, H)]) for q in range(4)], axis=0)

        term = half(k)
        for q in range(4):
            rows = pl.ds(q * Q, Q)
            part[s, rows] = dot(high[rows, mine], term) + dot(low[rows, mine], term)
        again(5)
        yield
        arrived(full_c.at[s, rows_of((1 - k) * 256, 256)], s, 9)
        term = half(1 - k)
        slots = [zh_out.at[s, 0], zh_out.at[s, 2], zh_out.at[s, 3], zh_out.at[s, 4]]
        for j in range(4):
            rows = rows_of((x + j) % 4 * Q, Q)
            slots[j][...] = fold(part[s, rows] + (dot(high[rows, his], term) + dot(low[rows, his], term)))
        for j in (2, 1, 3):
            push(slots[j], x_in.at[s, j - 1], s, 5, 10, xs[j - 1])
        again(6, 7)
        yield
        arrived(x_in.at[s], s, 10)
        zh_out[s, 0] = (zh_out[s, 0] + x_in[s, 0]) + (x_in[s, 1] + x_in[s, 2])
        first, second = pl.ds(0, H // 2), pl.ds(H // 2, H // 2)
        push(zh_out.at[s, 0, first], zh_in1.at[s, 0], s, 6, 11, zh_a)
        push(zh_out.at[s, 0, second], zh_in1.at[s, 1], s, 6, 12, zh_b)
        yield
        arrived(zh_in1.at[s, 0], s, 11)
        zh_out[s, 1, first] = zh_out[s, 0, first] + zh_in1[s, 0]
        push(zh_out.at[s, 1, first], zh_in2.at[s, 0], s, 7, 13, zh_b)
        arrived(zh_in1.at[s, 1], s, 12)
        zh_out[s, 1, second] = zh_out[s, 0, second] + zh_in1[s, 1]
        push(zh_out.at[s, 1, second], zh_in2.at[s, 1], s, 7, 13, zh_a)
        again(8)
        yield
        here = rows_of(x * H, H)
        arrived(zh_in2.at[s], s, 13)
        full_r[s, here] = zh_out[s, 1] + zh_in2[s].reshape(H, T)
        for j in (2, 1, 3):
            push(full_r.at[s, here], full_r.at[s, here], s, 8, 14, xs[j - 1])
        yield
        arrived(x_in.at[s], s, 14)

    def back_terms(p):
        s = 2 + p
        b = jnp.concatenate([operand(full_r[p, q * H : (q + 1) * H]) for q in range(4)], axis=0)
        for q in range(4):
            rows = rows_of((1 - k) * 512 + q * Q, Q)
            away[s, q * H : (q + 1) * H] = fold(dot(kth[rows, :], b) + dot(ktl[rows, :], b))
        send_away(s)
        for q in range(4):
            rows = rows_of(k * 512 + q * Q, Q)
            own[s, q * H : (q + 1) * H] = fold(dot(kth[rows, :], b) + dot(ktl[rows, :], b))

    def whole(p):
        yield from chain(p, 0, kh, kl)
        back_terms(p)
        yield from chain(p, 1, rth, rtl)

    def kernel_block(e):
        def run():
            if e == 0:
                loads[3].wait()
                loads[4].wait()
            cols = slice(e * 256, (e + 1) * 256)
            a, b = points[...], centers[cols, :]
            a_sq = jnp.sum(a * a, axis=1, keepdims=True)
            b_sq = across(jnp.ones((8, b.shape[1]), F32), b * b)[0:1]
            block = jnp.exp(-0.5 * ((a_sq + b_sq) - 2.0 * across(a, b)))
            kh[:, cols], kl[:, cols] = split(block)
            kth[cols, :], ktl[cols, :] = split(block.T)

        return run

    def factor_block(e):
        def run():
            cols = slice(e * 256, (e + 1) * 256)
            rth[:, cols], rtl[:, cols] = split(factor[cols, :].T)

        return run

    def norm(a):
        return jnp.sum(a * a, axis=0, keepdims=True)

    def first_norms():
        loads[5].wait()
        squares = [norm(full_r[p]) for p in (0, 1)]
        squares = [a + swap(a) for a in squares]
        predicted = jnp.where(first_lanes(1), squares[0], squares[1])
        small_start(0, jnp.concatenate([norm(residual[...]), norm(direction[...]), predicted], axis=1))

    loads[0].wait()
    pair = jnp.concatenate(split(direction[...]), axis=1)

    def mapped(base, target):
        for q in range(4):
            high, low = split(factor[rows_of(base * 512 + q * Q, Q), :])
            both = dot(high, pair) + dot(low, pair)
            both = both[:, :T] + both[:, T:]
            for p in (0, 1):
                target[p, q * H : (q + 1) * H] = pack(both, p)

    loads[1].wait()
    mapped(1 - k, away)
    pl.semaphore_wait(barrier, len(peers))
    for p in (0, 1):
        send_away(p)
    loads[2].wait()
    mapped(k, own)

    chains = [whole(0), whole(1)]
    extra = {
        1: [kernel_block(0), kernel_block(1)],
        2: [kernel_block(2), kernel_block(3)],
        6: [factor_block(0), factor_block(1)],
        7: [factor_block(2), factor_block(3)],
        10: [first_norms],
    }
    for step in range(18):
        for p in (0, 1):
            next(chains[p])
        for run in extra.get(step, []):
            run()

    sums = small_end(0)
    norm_now = sums[:, :T]
    step_size = norm_now / (sums[:, 2 * T :] + ridge_weight * sums[:, T : 2 * T])
    line[0] = step_size
    outs = [pltpu.make_async_copy(line.at[0], step_out, local.at[6])]
    outs[0].start()
    for p in (0, 1):
        for unused in chains[p]:
            pass
    total = jnp.zeros((1, T), F32)
    for q in range(4):
        rows, packed = slice(q * Q, (q + 1) * Q), pl.ds(q * H, H)
        quarter = unpack(full_r[2, packed], full_r[3, packed])
        image[rows] = quarter
        total = total + norm(residual[rows] - step_size * (quarter + ridge_weight * direction[rows]))
    small_start(1, total)
    outs.append(pltpu.make_async_copy(image, image_, local.at[7]))
    outs[1].start()
    for p in (0, 1):
        for phase in range(9):
            sent(2 + p, phase)
    for out in outs:
        out.wait()
    line[1] = small_end(1) / norm_now
    last = pltpu.make_async_copy(line.at[1], ratio_out, local.at[8])
    last.start()
    last.wait()


def body(points, centers, factor, solution_, residual, direction):
    anywhere = pl.BlockSpec(memory_space=pl.ANY)
    dma = pltpu.SemaphoreType.DMA
    v = lambda *shape: pltpu.VMEM(shape, F32)
    h = lambda *shape: pltpu.VMEM(shape, BF16)
    image, step_size, ratio = pl.pallas_call(
        kernel,
        name="cg_iteration",
        out_shape=(jax.ShapeDtypeStruct(direction.shape, F32), jax.ShapeDtypeStruct((1, T), F32), jax.ShapeDtypeStruct((1, T), F32)),
        in_specs=[anywhere] * 5,
        out_specs=(anywhere,) * 3,
        scratch_shapes=[
            v(512, 256), v(1024, 256), v(1024, 512), v(512, T), v(512, T), v(512, T),
            v(4, 256, T), v(4, 256, T), v(4, 256, T), v(4, 3, H, T), v(4, 4, H, T), v(4, 512, T),
            v(4, 512, T), v(4, 3, H, T), v(4, 5, H, T), v(4, 2, H // 2, T), v(4, 2, H // 2, T), v(4, 256, T),
            h(512, 1024), h(512, 1024), h(1024, 512), h(1024, 512), h(512, 1024), h(512, 1024),
            v(32, 1, 3 * T), v(32, 1, T), v(2, 1, T),
            dma((2, 9)), dma((4, 15)), dma((2,)), dma((2,)), dma((9,)),
        ],
        compiler_params=pltpu.CompilerParams(collective_id=0, has_side_effects=True, vmem_limit_bytes=60 * 2**20),
    )(points, centers, factor, residual, direction)
    new_solution = solution_ + step_size * direction
    new_residual = residual - step_size * (image + ridge_weight * direction)
    return new_solution, new_residual, new_residual + ratio * direction


def solution(mesh):
    return jax.shard_map(
        body,
        mesh=mesh,
        in_specs=(
            P("rows", None),
            P("cols", None),
            P("cols", "rows"),
            P("rows", None),
            P("rows", None),
            P("rows", None),
        ),
        out_specs=(P("rows", None), P("rows", None), P("rows", None)),
        check_vma=False,
    )
```

time: 100 us -> 93.9 us (0.939)
  Pallas kernels: 97.6 us -> 91.1 us
    pallas_call x1, Pallas kernels: 97.6 us -> 91.1 us  [body(): pl.pallas_call(kernel, name='cg_iteration', out_shape=(jax.ShapeDtypeStru...]
where the time goes in v3:
time: 93.9 us; the launch traced here: 93.7 us
  Pallas kernels  91.1 us (97%)
  other arithmetic  1.89 us (2%)
    pallas_call x1, Pallas kernels, body(): pl.pallas_call(kernel, name='cg_iteration', out_shape=(jax.ShapeDtypeStru...  91.1 us
    add x1, other arithmetic, body(): return (new_solution, new_residual, new_residual + ratio * direction)  1.89 us

profile of v3, /device:TPU:1, one launch (start us, length us, event | category | flops | bytes accessed | tf_op | source)
XLA Modules:
  0.0 93.7 jit_solution(2136798440587108133)
XLA Ops:
  0.6 0.0 copy-start
  0.6 0.0 copy-start.1
  0.7 0.0 copy-start.2
  0.7 91.1 %cg_iteration.1 = (f32[512,128]{1,0:T(8,128)}, f32[1,128]{1,0:T(1,128)}, f32[1,128]{1,0:T(1,128)}) custom-call(f32[512,256]{1,0:T(8,128)} %points_.1, f32[1024,256]{1,0:T(8,128)} %centers_.1, f32[1024,512]{1,0:T(8,128)} %factor_.1, f32[512,128]{1,0:T(8,128)} %residual_.1, f32[512,128]{1,0:T(8,128)} %direction_.1), custom_call_target="tpu_custom_call" | custom-call | tf_op jit(solution)/shard_map/cg_iteration/pallas_call | solution.py:349
  91.8 0.0 copy-done
  91.8 0.0 copy-done.1
  91.8 0.0 copy-done.2
  91.8 1.9 %multiply_add_fusion = (f32[512,128]{1,0:T(8,128)}, f32[512,128]{1,0:T(8,128)}, f32[512,128]{1,0:T(8,128)}) fusion(f32[512,128]{1,0:T(8,128)S(1)} %copy-done, f32[128]{0:T(128)} %bitcast.3, f32[512,128]{1,0:T(8,128)S(1)} %copy-done.1, f32[512,128]{1,0:T(8,128)} %get-tuple-element.7, f32[128]{0:T(128)} %bitcast.2, f32[512,128]{1,0:T(8,128)S(1)} %copy-done.2), kind=kLoop, calls=%fused_computation | loop fusion | flops 524288 | bytes 1836032 | tf_op jit(solution)/shard_map/add | solution.py:367
Async XLA Ops:
  0.6 91.2 %copy-start = (f32[512,128]{1,0:T(8,128)S(1)}, f32[512,128]{1,0:T(8,128)}, u32[]{:S(2)}) copy-start(f32[512,128]{1,0:T(8,128)} %direction_.1) | copy-start | bytes 786436
  0.6 91.2 %copy-start.1 = (f32[512,128]{1,0:T(8,128)S(1)}, f32[512,128]{1,0:T(8,128)}, u32[]{:S(2)}) copy-start(f32[512,128]{1,0:T(8,128)} %residual_.1) | copy-start | bytes 786436
  0.7 91.2 %copy-start.2 = (f32[512,128]{1,0:T(8,128)S(1)}, f32[512,128]{1,0:T(8,128)}, u32[]{:S(2)}) copy-start(f32[512,128]{1,0:T(8,128)} %param.9) | copy-start | bytes 786436

commit v4 on v3

--- a/solution.py
+++ b/solution.py
@@ -72,24 +72,30 @@
     away, own, core_in, a_in, b_in, full_c,
     part, x_in, zh_out, zh_in1, zh_in2, full_r,
     kh, kl, kth, ktl, rth, rtl,
-    small_a, small_b, line,
+    small_a, small_b, small_x, line,
     send, recv, small_send, small_recv, local,
 ):
     r, c = lax.axis_index("rows"), lax.axis_index("cols")
-    y, zl, k = r // 8, (r // 2) % 4, r % 2
-    x, zh = c // 4, c % 4
+    y, k = lax.div(r, 8), lax.rem(r, 2)
+    zl = lax.rem(lax.div(r, 2), 4)
+    x, zh = lax.div(c, 4), lax.rem(c, 4)
+
+    def turn(v, j):
+        return v if isinstance(j, int) and j == 0 else lax.rem(v + j, 4)
 
     def at(y_=None, zl_=None, k_=None, x_=None, zh_=None):
         pick = lambda new, old: old if new is None else new
         return (pick(y_, y) * 8 + pick(zl_, zl) * 2 + pick(k_, k), pick(x_, x) * 4 + pick(zh_, zh))
 
     sibling = at(k_=1 - k)
-    ys = [at(y_=(y + j) % 4) for j in (1, 2, 3)]
-    zls = [at(zl_=(zl + j) % 4) for j in (1, 2, 3)]
-    xs = [at(x_=(x + j) % 4) for j in (1, 2, 3)]
-    zh_a = at(zh_=zh + 1 - 2 * (zh % 2))
-    zh_b = at(zh_=(zh + 3 - 2 * (zh % 2)) % 4)
-    column = [at((y + i) % 4, (zl + j) % 4, (k + e) % 2) for i in (2, 1, 3, 0) for j in (2, 1, 3, 0) for e in (1, 0)][:-1]
+    ys = [at(y_=turn(y, j)) for j in (1, 2, 3)]
+    zls = [at(zl_=turn(zl, j)) for j in (1, 2, 3)]
+    xs = [at(x_=turn(x, j)) for j in (1, 2, 3)]
+    zh_a = at(zh_=zh + 1 - 2 * lax.rem(zh, 2))
+    zh_b = at(zh_=turn(zh, 3 - 2 * lax.rem(zh, 2)))
+    column = [
+        at(turn(y, i), turn(zl, j), 1 - k if e else k) for i in (2, 1, 3, 0) for j in (2, 1, 3, 0) for e in (1, 0)
+    ][:-1]
 
     here_half, there_half = rows_of(k * 512, 512), rows_of((1 - k) * 512, 512)
     loads = [
@@ -149,7 +155,7 @@
             sent(s, 0)
         for q in range(4):
             rows = pl.ds(q * H, H)
-            push(away.at[s, rows], core_in.at[s, rows], s, 0, q, sibling)
+            push(away.at[s, rows], core_in.at[s, rows], s, 0, 0, sibling)
 
     def chain(p, n, high, low):
         s = 2 * n + p
@@ -161,33 +167,30 @@
 
         yield
         again(1)
-        for j in (2, 1, 3, 0):
-            q = (a + j) % 4
-            rows = rows_of(q * H, H)
-            arrived(core_in.at[s, rows], s, q)
-            own[s, rows] = own[s, rows] + core_in[s, rows]
-            if j:
-                push(own.at[s, rows], a_in.at[s, j - 1], s, 1, 4, a_devices[j - 1])
+        arrived(core_in.at[s], s, 0)
+        own[s] = own[s] + core_in[s]
+        for j in (2, 1, 3):
+            push(own.at[s, rows_of((a + j) % 4 * H, H)], a_in.at[s, j - 1], s, 1, 1, a_devices[j - 1])
         again(2)
         yield
         mine = rows_of(a * H, H)
-        arrived(a_in.at[s], s, 4)
+        arrived(a_in.at[s], s, 1)
         b_in[s, b] = (own[s, mine] + a_in[s, 0]) + (a_in[s, 1] + a_in[s, 2])
         for j in (2, 1, 3):
-            push(b_in.at[s, b], b_in.at[s, b], s, 2, 5, b_devices[j - 1])
+            push(b_in.at[s, b], b_in.at[s, b], s, 2, 2, b_devices[j - 1])
         again(3, 4)
         yield
-        arrived(a_in.at[s], s, 5)
+        arrived(a_in.at[s], s, 2)
         here = rows_of(k * 256 + a * H, H)
         full_c[s, here] = (b_in[s, 0] + b_in[s, 1]) + (b_in[s, 2] + b_in[s, 3])
         for j in (2, 1, 3):
-            push(full_c.at[s, here], full_c.at[s, here], s, 3, 6 + j - 1, a_devices[j - 1])
-        push(full_c.at[s, here], full_c.at[s, here], s, 4, 9, sibling)
+            push(full_c.at[s, here], full_c.at[s, here], s, 3, 3 + j - 1, a_devices[j - 1])
+        push(full_c.at[s, here], full_c.at[s, here], s, 4, 6, sibling)
         yield
         for j in (1, 3, 2):
             there = rows_of(k * 256 + (a + 4 - j) % 4 * H, H)
-            arrived(full_c.at[s, there], s, 6 + j - 1)
-            push(full_c.at[s, there], full_c.at[s, there], s, 4, 9, sibling)
+            arrived(full_c.at[s, there], s, 3 + j - 1)
+            push(full_c.at[s, there], full_c.at[s, there], s, 4, 6, sibling)
         mine, his = rows_of(k * 512, 512), rows_of((1 - k) * 512, 512)
 
         def half(base):
@@ -199,37 +202,39 @@
             part[s, rows] = dot(high[rows, mine], term) + dot(low[rows, mine], term)
         again(5)
         yield
-        arrived(full_c.at[s, rows_of((1 - k) * 256, 256)], s, 9)
+        arrived(full_c.at[s, rows_of((1 - k) * 256, 256)], s, 6)
         term = half(1 - k)
         slots = [zh_out.at[s, 0], zh_out.at[s, 2], zh_out.at[s, 3], zh_out.at[s, 4]]
         for j in range(4):
             rows = rows_of((x + j) % 4 * Q, Q)
             slots[j][...] = fold(part[s, rows] + (dot(high[rows, his], term) + dot(low[rows, his], term)))
         for j in (2, 1, 3):
-            push(slots[j], x_in.at[s, j - 1], s, 5, 10, xs[j - 1])
+            push(slots[j], x_in.at[s, j - 1], s, 5, 7, xs[j - 1])
         again(6, 7)
         yield
-        arrived(x_in.at[s], s, 10)
+        arrived(x_in.at[s], s, 7)
         zh_out[s, 0] = (zh_out[s, 0] + x_in[s, 0]) + (x_in[s, 1] + x_in[s, 2])
         first, second = pl.ds(0, H // 2), pl.ds(H // 2, H // 2)
-        push(zh_out.at[s, 0, first], zh_in1.at[s, 0], s, 6, 11, zh_a)
-        push(zh_out.at[s, 0, second], zh_in1.at[s, 1], s, 6, 12, zh_b)
-        yield
-        arrived(zh_in1.at[s, 0], s, 11)
+        push(zh_out.at[s, 0, first], zh_in1.at[s, 0], s, 6, 8, zh_a)
+        push(zh_out.at[s, 0, second], zh_in1.at[s, 1], s, 6, 9, zh_b)
+        yield
+        arrived(zh_in1.at[s, 0], s, 8)
         zh_out[s, 1, first] = zh_out[s, 0, first] + zh_in1[s, 0]
-        push(zh_out.at[s, 1, first], zh_in2.at[s, 0], s, 7, 13, zh_b)
-        arrived(zh_in1.at[s, 1], s, 12)
+        push(zh_out.at[s, 1, first], zh_in2.at[s, 0], s, 7, 10, zh_b)
+        arrived(zh_in1.at[s, 1], s, 9)
         zh_out[s, 1, second] = zh_out[s, 0, second] + zh_in1[s, 1]
-        push(zh_out.at[s, 1, second], zh_in2.at[s, 1], s, 7, 13, zh_a)
+        push(zh_out.at[s, 1, second], zh_in2.at[s, 1], s, 7, 10, zh_a)
         again(8)
         yield
         here = rows_of(x * H, H)
-        arrived(zh_in2.at[s], s, 13)
+        arrived(zh_in2.at[s], s, 10)
         full_r[s, here] = zh_out[s, 1] + zh_in2[s].reshape(H, T)
-        for j in (2, 1, 3):
-            push(full_r.at[s, here], full_r.at[s, here], s, 8, 14, xs[j - 1])
-        yield
-        arrived(x_in.at[s], s, 14)
+        if s == 3:
+            yield
+        for j in (2, 1, 3):
+            push(full_r.at[s, here], full_r.at[s, here], s, 8, 11, xs[j - 1])
+        yield
+        arrived(x_in.at[s], s, 11)
 
     def back_terms(p):
         s = 2 + p
@@ -307,7 +312,7 @@
         10: [first_norms],
     }
     for step in range(18):
-        for p in (0, 1):
+        for p in (1, 0) if step in (3, 12) else (0, 1):
             next(chains[p])
         for run in extra.get(step, []):
             run()
@@ -315,19 +320,26 @@
     sums = small_end(0)
     norm_now = sums[:, :T]
     step_size = norm_now / (sums[:, 2 * T :] + ridge_weight * sums[:, T : 2 * T])
+    quarter, packed = rows_of(x * Q, Q), rows_of(x * H, H)
+    fresh = residual[quarter, :] - step_size * (
+        unpack(full_r[2, packed], full_r[3, packed]) + ridge_weight * direction[quarter, :]
+    )
+    small_x[x] = norm(fresh)
+    for device in xs:
+        copy(small_x.at[x], small_x.at[x], small_send.at[2], small_recv.at[2], device).start()
+    next(chains[1])
     line[0] = step_size
     outs = [pltpu.make_async_copy(line.at[0], step_out, local.at[6])]
     outs[0].start()
+    like = small_x.at[pl.ds(0, 3)]
+    copy(like, like, small_send.at[2], small_recv.at[2], sibling).wait()
+    small_start(1, jnp.sum(small_x[...], axis=0))
     for p in (0, 1):
         for unused in chains[p]:
             pass
-    total = jnp.zeros((1, T), F32)
     for q in range(4):
-        rows, packed = slice(q * Q, (q + 1) * Q), pl.ds(q * H, H)
-        quarter = unpack(full_r[2, packed], full_r[3, packed])
-        image[rows] = quarter
-        total = total + norm(residual[rows] - step_size * (quarter + ridge_weight * direction[rows]))
-    small_start(1, total)
+        packed = pl.ds(q * H, H)
+        image[q * Q : (q + 1) * Q] = unpack(full_r[2, packed], full_r[3, packed])
     outs.append(pltpu.make_async_copy(image, image_, local.at[7]))
     outs[1].start()
     for p in (0, 1):
@@ -357,8 +369,8 @@
             v(4, 256, T), v(4, 256, T), v(4, 256, T), v(4, 3, H, T), v(4, 4, H, T), v(4, 512, T),
             v(4, 512, T), v(4, 3, H, T), v(4, 5, H, T), v(4, 2, H // 2, T), v(4, 2, H // 2, T), v(4, 256, T),
             h(512, 1024), h(512, 1024), h(1024, 512), h(1024, 512), h(512, 1024), h(512, 1024),
-            v(32, 1, 3 * T), v(32, 1, T), v(2, 1, T),
-            dma((2, 9)), dma((4, 15)), dma((2,)), dma((2,)), dma((9,)),
+            v(32, 1, 3 * T), v(32, 1, T), v(4, 1, T), v(2, 1, T),
+            dma((2, 9)), dma((4, 12)), dma((3,)), dma((3,)), dma((9,)),
         ],
         compiler_params=pltpu.CompilerParams(collective_id=0, has_side_effects=True, vmem_limit_bytes=60 * 2**20),
     )(points, centers, factor, residual, direction)

time: 93.9 us -> 94.8 us (level)
  no operation moved by 1% of the time
where the time goes in v4:
time: 94.8 us; the launch traced here: 94.6 us
  Pallas kernels  92 us (97%)
  other arithmetic  1.89 us (2%)
    pallas_call x1, Pallas kernels, body(): pl.pallas_call(kernel, name='cg_iteration', out_shape=(jax.ShapeDtypeStru...  92 us

profile of v4, /device:TPU:1, one launch (start us, length us, event | category | flops | bytes accessed | tf_op | source)
XLA Modules:
  0.0 94.6 jit_solution(9000010972504431493)
XLA Ops:
  0.6 0.0 copy-start
  0.6 0.0 copy-start.1
  0.7 0.0 copy-start.2
  0.7 92.0 %cg_iteration.1 = (f32[512,128]{1,0:T(8,128)}, f32[1,128]{1,0:T(1,128)}, f32[1,128]{1,0:T(1,128)}) custom-call(f32[512,256]{1,0:T(8,128)} %points_.1, f32[1024,256]{1,0:T(8,128)} %centers_.1, f32[1024,512]{1,0:T(8,128)} %factor_.1, f32[512,128]{1,0:T(8,128)} %residual_.1, f32[512,128]{1,0:T(8,128)} %direction_.1), custom_call_target="tpu_custom_call" | custom-call | tf_op jit(solution)/shard_map/cg_iteration/pallas_call | solution.py:361
  92.7 0.0 copy-done
  92.7 0.0 copy-done.1
  92.7 0.0 copy-done.2
  92.7 1.9 %multiply_add_fusion = (f32[512,128]{1,0:T(8,128)}, f32[512,128]{1,0:T(8,128)}, f32[512,128]{1,0:T(8,128)}) fusion(f32[512,128]{1,0:T(8,128)S(1)} %copy-done, f32[128]{0:T(128)} %bitcast.3, f32[512,128]{1,0:T(8,128)S(1)} %copy-done.1, f32[512,128]{1,0:T(8,128)} %get-tuple-element.7, f32[128]{0:T(128)} %bitcast.2, f32[512,128]{1,0:T(8,128)S(1)} %copy-done.2), kind=kLoop, calls=%fused_computation | loop fusion | flops 524288 | bytes 1836032 | tf_op jit(solution)/shard_map/add | solution.py:379
Async XLA Ops:
  0.6 92.1 %copy-start = (f32[512,128]{1,0:T(8,128)S(1)}, f32[512,128]{1,0:T(8,128)}, u32[]{:S(2)}) copy-start(f32[512,128]{1,0:T(8,128)} %direction_.1) | copy-start | bytes 786436
  0.6 92.1 %copy-start.1 = (f32[512,128]{1,0:T(8,128)S(1)}, f32[512,128]{1,0:T(8,128)}, u32[]{:S(2)}) copy-start(f32[512,128]{1,0:T(8,128)} %residual_.1) | copy-start | bytes 786436
  0.7 92.1 %copy-start.2 = (f32[512,128]{1,0:T(8,128)S(1)}, f32[512,128]{1,0:T(8,128)}, u32[]{:S(2)}) copy-start(f32[512,128]{1,0:T(8,128)} %param.9) | copy-start | bytes 786436

commit v5 on v4

--- a/solution.py
+++ b/solution.py
@@ -114,7 +114,7 @@
     loads[0].start()
     loads[1].start()
 
-    peers = [zh_a, zh_b] + column + xs
+    peers = [zh_a, zh_b] + zls + ys + xs + [sibling]
     barrier = pltpu.get_barrier_semaphore()
     for p in peers:
         pl.semaphore_signal(barrier, inc=1, device_id=p, device_id_type=MESH)

time: 94.8 us -> 94.1 us (level)
  no operation moved by 1% of the time
where the time goes in v5:
time: 94.1 us; the launch traced here: 93.9 us
  Pallas kernels  91.3 us (97%)
  other arithmetic  1.89 us (2%)
    pallas_call x1, Pallas kernels, body(): pl.pallas_call(kernel, name='cg_iteration', out_shape=(jax.ShapeDtypeStru...  91.3 us
    add x1, other arithmetic, body(): return (new_solution, new_residual, new_residual + ratio * direction)  1.89 us

profile of v5, /device:TPU:1, one launch (start us, length us, event | category | flops | bytes accessed | tf_op | source)
XLA Modules:
  0.0 93.9 jit_solution(17138099466129590292)
XLA Ops:
  0.6 0.0 copy-start
  0.6 0.0 copy-start.1
  0.7 0.0 copy-start.2
  0.7 91.3 %cg_iteration.1 = (f32[512,128]{1,0:T(8,128)}, f32[1,128]{1,0:T(1,128)}, f32[1,128]{1,0:T(1,128)}) custom-call(f32[512,256]{1,0:T(8,128)} %points_.1, f32[1024,256]{1,0:T(8,128)} %centers_.1, f32[1024,512]{1,0:T(8,128)} %factor_.1, f32[512,128]{1,0:T(8,128)} %residual_.1, f32[512,128]{1,0:T(8,128)} %direction_.1), custom_call_target="tpu_custom_call" | custom-call | tf_op jit(solution)/shard_map/cg_iteration/pallas_call | solution.py:361
  92.0 0.0 copy-done
  92.0 0.0 copy-done.1
  92.0 0.0 copy-done.2
  92.0 1.9 %multiply_add_fusion = (f32[512,128]{1,0:T(8,128)}, f32[512,128]{1,0:T(8,128)}, f32[512,128]{1,0:T(8,128)}) fusion(f32[512,128]{1,0:T(8,128)S(1)} %copy-done, f32[128]{0:T(128)} %bitcast.3, f32[512,128]{1,0:T(8,128)S(1)} %copy-done.1, f32[512,128]{1,0:T(8,128)} %get-tuple-element.7, f32[128]{0:T(128)} %bitcast.2, f32[512,128]{1,0:T(8,128)S(1)} %copy-done.2), kind=kLoop, calls=%fused_computation | loop fusion | flops 524288 | bytes 1836032 | tf_op jit(solution)/shard_map/add | solution.py:379
Async XLA Ops:
  0.6 91.4 %copy-start = (f32[512,128]{1,0:T(8,128)S(1)}, f32[512,128]{1,0:T(8,128)}, u32[]{:S(2)}) copy-start(f32[512,128]{1,0:T(8,128)} %direction_.1) | copy-start | bytes 786436
  0.6 91.4 %copy-start.1 = (f32[512,128]{1,0:T(8,128)S(1)}, f32[512,128]{1,0:T(8,128)}, u32[]{:S(2)}) copy-start(f32[512,128]{1,0:T(8,128)} %residual_.1) | copy-start | bytes 786436
  0.7 91.4 %copy-start.2 = (f32[512,128]{1,0:T(8,128)S(1)}, f32[512,128]{1,0:T(8,128)}, u32[]{:S(2)}) copy-start(f32[512,128]{1,0:T(8,128)} %param.9) | copy-start | bytes 786436

commit v6 on v5

--- a/solution.py
+++ b/solution.py
@@ -166,6 +166,8 @@
                 sent(s, phase)
 
         yield
+        if n:
+            own_back_terms(p)
         again(1)
         arrived(core_in.at[s], s, 0)
         own[s] = own[s] + core_in[s]
@@ -205,11 +207,16 @@
         arrived(full_c.at[s, rows_of((1 - k) * 256, 256)], s, 6)
         term = half(1 - k)
         slots = [zh_out.at[s, 0], zh_out.at[s, 2], zh_out.at[s, 3], zh_out.at[s, 4]]
-        for j in range(4):
+
+        def finish(j):
             rows = rows_of((x + j) % 4 * Q, Q)
             slots[j][...] = fold(part[s, rows] + (dot(high[rows, his], term) + dot(low[rows, his], term)))
+
+        for j in (2, 1, 3):
+            finish(j)
         for j in (2, 1, 3):
             push(slots[j], x_in.at[s, j - 1], s, 5, 7, xs[j - 1])
+        finish(0)
         again(6, 7)
         yield
         arrived(x_in.at[s], s, 7)
@@ -236,20 +243,21 @@
         yield
         arrived(x_in.at[s], s, 11)
 
-    def back_terms(p):
-        s = 2 + p
+    def back_terms(p, base):
         b = jnp.concatenate([operand(full_r[p, q * H : (q + 1) * H]) for q in range(4)], axis=0)
         for q in range(4):
-            rows = rows_of((1 - k) * 512 + q * Q, Q)
-            away[s, q * H : (q + 1) * H] = fold(dot(kth[rows, :], b) + dot(ktl[rows, :], b))
-        send_away(s)
-        for q in range(4):
-            rows = rows_of(k * 512 + q * Q, Q)
-            own[s, q * H : (q + 1) * H] = fold(dot(kth[rows, :], b) + dot(ktl[rows, :], b))
+            rows = rows_of(base * 512 + q * Q, Q)
+            yield q, fold(dot(kth[rows, :], b) + dot(ktl[rows, :], b))
+
+    def own_back_terms(p):
+        for q, term in back_terms(p, k):
+            own[2 + p, q * H : (q + 1) * H] = term
 
     def whole(p):
         yield from chain(p, 0, kh, kl)
-        back_terms(p)
+        for q, term in back_terms(p, 1 - k):
+            away[2 + p, q * H : (q + 1) * H] = term
+        send_away(2 + p)
         yield from chain(p, 1, rth, rtl)
 
     def kernel_block(e):
@@ -312,7 +320,7 @@
         10: [first_norms],
     }
     for step in range(18):
-        for p in (1, 0) if step in (3, 12) else (0, 1):
+        for p in (0, 1):
             next(chains[p])
         for run in extra.get(step, []):
             run()

time: 94.1 us -> 94 us (level)
  no operation moved by 1% of the time
where the time goes in v6:
time: 94 us; the launch traced here: 93.9 us
  Pallas kernels  91.3 us (97%)
  other arithmetic  1.89 us (2%)
    pallas_call x1, Pallas kernels, body(): pl.pallas_call(kernel, name='cg_iteration', out_shape=(jax.ShapeDtypeStru...  91.3 us
    add x1, other arithmetic, body(): return (new_solution, new_residual, new_residual + ratio * direction)  1.89 us

profile of v6, /device:TPU:1, one launch (start us, length us, event | category | flops | bytes accessed | tf_op | source)
XLA Modules:
  0.0 93.9 jit_solution(6967915822150381958)
XLA Ops:
  0.6 0.0 copy-start
  0.6 0.0 copy-start.1
  0.7 0.0 copy-start.2
  0.7 91.3 %cg_iteration.1 = (f32[512,128]{1,0:T(8,128)}, f32[1,128]{1,0:T(1,128)}, f32[1,128]{1,0:T(1,128)}) custom-call(f32[512,256]{1,0:T(8,128)} %points_.1, f32[1024,256]{1,0:T(8,128)} %centers_.1, f32[1024,512]{1,0:T(8,128)} %factor_.1, f32[512,128]{1,0:T(8,128)} %residual_.1, f32[512,128]{1,0:T(8,128)} %direction_.1), custom_call_target="tpu_custom_call" | custom-call | tf_op jit(solution)/shard_map/cg_iteration/pallas_call | solution.py:369
  92.0 0.0 copy-done
  92.0 0.0 copy-done.1
  92.0 0.0 copy-done.2
  92.0 1.9 %multiply_add_fusion = (f32[512,128]{1,0:T(8,128)}, f32[512,128]{1,0:T(8,128)}, f32[512,128]{1,0:T(8,128)}) fusion(f32[512,128]{1,0:T(8,128)S(1)} %copy-done, f32[128]{0:T(128)} %bitcast.3, f32[512,128]{1,0:T(8,128)S(1)} %copy-done.1, f32[512,128]{1,0:T(8,128)} %get-tuple-element.7, f32[128]{0:T(128)} %bitcast.2, f32[512,128]{1,0:T(8,128)S(1)} %copy-done.2), kind=kLoop, calls=%fused_computation | loop fusion | flops 524288 | bytes 1836032 | tf_op jit(solution)/shard_map/add | solution.py:387
Async XLA Ops:
  0.6 91.3 %copy-start = (f32[512,128]{1,0:T(8,128)S(1)}, f32[512,128]{1,0:T(8,128)}, u32[]{:S(2)}) copy-start(f32[512,128]{1,0:T(8,128)} %direction_.1) | copy-start | bytes 786436
  0.6 91.3 %copy-start.1 = (f32[512,128]{1,0:T(8,128)S(1)}, f32[512,128]{1,0:T(8,128)}, u32[]{:S(2)}) copy-start(f32[512,128]{1,0:T(8,128)} %residual_.1) | copy-start | bytes 786436
  0.7 91.3 %copy-start.2 = (f32[512,128]{1,0:T(8,128)S(1)}, f32[512,128]{1,0:T(8,128)}, u32[]{:S(2)}) copy-start(f32[512,128]{1,0:T(8,128)} %param.9) | copy-start | bytes 786436
